TPU v7x, 512 devices: a whole 4x8x8 slice. The times are simulated.
512 devices in a mesh: ta: 4 (over z_hi), ha: 8 (over x, core), wa: 16 (over y, z_lo).
Axes of the slice: x: 4, y: 8, z: 8 (z_hi: 4, z_lo: 2; z = z_hi * 2 + z_lo), core: 2. Of those that a mesh axis runs over, the one named last changes fastest.
Arguments:
- query_in: bfloat16 [12, 64, 128, 256], P('ta', 'ha', 'wa'), may hold values from -24 to 24
- key_in: bfloat16 [12, 64, 128, 256], P('ta', 'ha', 'wa'), may hold values from -24 to 24
- value_in: bfloat16 [12, 64, 128, 256], P('ta', 'ha', 'wa'), may hold values from -6 to 6
- cotangent: bfloat16 [12, 64, 128, 256], P('ta', 'ha', 'wa'), may hold values from -6 to 6
Outputs:
- attended: bfloat16 [12, 64, 128, 256], P('ta', 'ha', 'wa')
- grad_query: bfloat16 [12, 64, 128, 256], P('ta', 'ha', 'wa')
- grad_key: bfloat16 [12, 64, 128, 256], P('ta', 'ha', 'wa')
- grad_value: bfloat16 [12, 64, 128, 256], P('ta', 'ha', 'wa')
All inputs are finite; a program needn't handle non-finite values.
Results may differ from a plain program's by a relative error of at most 0.035.
Values may be sent and summed in bfloat16 or wider, within the bound.
A program may use at most 128 MiB of HBM per device.

v0:
```python
import functools

import jax
import jax.numpy as jnp
import numpy as np
from jax import lax
from jax.experimental import pallas as pl
from jax.experimental.pallas import tpu as pltpu
from jax.sharding import PartitionSpec as P

DH = 128
HEADS = 2
TILE = 8
FRAMES = 3
CELLS = FRAMES * TILE * TILE
CHAN = HEADS * DH
PAIR = 2 * CELLS
QUERIES = 4 * CELLS
SCALE = DH ** (-0.5)
EXP2_SCALE = SCALE * 1.4426950408889634
BIG = 1e30
POS = {2: 0, 1: 1, 3: 2, 0: 3}


def ahead(axis, step):
    size = lax.axis_size(axis)
    return lax.rem(lax.axis_index(axis) + (step + size), size)


def dot_nt(a, b):
    return lax.dot_general(a, b, (((1,), (1,)), ((), ())), preferred_element_type=jnp.float32)


def dot_tn(a, b):
    return lax.dot_general(a, b, (((0,), (0,)), ((), ())), preferred_element_type=jnp.float32)


def dot_nn(a, b):
    return lax.dot_general(a, b, (((1,), (0,)), ((), ())), preferred_element_type=jnp.float32)


def turn(block, cosine, sine, direction):
    lane = lax.broadcasted_iota(jnp.int32, (CELLS, DH), 1)
    nxt = pltpu.roll(block, DH - 1, 1)
    prv = pltpu.roll(block, 1, 1)
    swapped = jnp.where(lane % 2 == 0, -nxt, prv)
    return block * cosine + swapped * (direction * sine)


def head(idx):
    return pl.ds(idx * DH, DH)


def kernel(
    freq_ref, q_ref, k_ref, v_ref, g_ref,
    o_ref, dq_ref, dk_ref, dv_ref,
    kv, qs, gs, cos_tab, sin_tab, scores, probs, dsc, acc_t, dq_t, mrow,
    osend, orecv, lsend, lrecv, ssend, srecv, dqsend, dqrecv,
    part, hrecv, wsend, wrecv,
    halo_s, halo_r, ta_s, ta_r, o_s, o_r, l_s, l_r, st_s, st_r, dq_s, dq_r, h_s, h_r, w_s, w_r,
):
    t_pos, h_pos, w_pos = lax.axis_index("ta"), lax.axis_index("ha"), lax.axis_index("wa")
    h_size, w_size = lax.axis_size("ha"), lax.axis_size("wa")

    barrier = pltpu.get_barrier_semaphore()
    partners = [{"ha": ahead("ha", 1)}, {"ha": ahead("ha", -1)}, {"wa": ahead("wa", 1)}, {"wa": ahead("wa", -1)}]
    partners += [{"ta": ahead("ta", r)} for r in (1, 2, 3)]
    for partner in partners:
        pl.semaphore_signal(barrier, inc=1, device_id=partner, device_id_type=pl.DeviceIdType.MESH)

    lane = lax.broadcasted_iota(jnp.int32, (TILE, DH), 1)
    sub = lax.broadcasted_iota(jnp.int32, (TILE, DH), 0)
    in_time = lane < DH // 8
    in_row = lane < DH // 8 + (DH - DH // 8) // 2
    start = jnp.where(in_time, t_pos * FRAMES, jnp.where(in_row, h_pos * TILE, w_pos * TILE))
    angle = (start + sub).astype(jnp.float32) * freq_ref[...]
    for table, value in ((cos_tab, jnp.cos(angle)), (sin_tab, jnp.sin(angle))):
        for frame in range(FRAMES):
            for row in range(TILE):
                table[pl.ds((frame * TILE + row) * TILE, TILE), :] = jnp.where(
                    in_time,
                    jnp.broadcast_to(value[frame : frame + 1], (TILE, DH)),
                    jnp.where(in_row, jnp.broadcast_to(value[row : row + 1], (TILE, DH)), value),
                )
    own = pl.ds(POS[0] * CELLS, CELLS)
    for idx in range(HEADS):
        cosine, sine = cos_tab[...], sin_tab[...]
        kv[4, 0, :, head(idx)] = turn(k_ref[:, head(idx)].astype(jnp.float32), cosine, sine, 1.0).astype(jnp.bfloat16)
        qs[own, head(idx)] = turn(q_ref[:, head(idx)].astype(jnp.float32), cosine, sine, 1.0).astype(jnp.bfloat16)
    kv[4, 1] = v_ref[...]
    gs[own, :] = g_ref[...]

    pl.semaphore_wait(barrier, len(partners))

    def remote(src, dst, send, recv, device):
        return pltpu.make_async_remote_copy(
            src_ref=src, dst_ref=dst, send_sem=send, recv_sem=recv,
            device_id=device, device_id_type=pl.DeviceIdType.MESH,
        )

    def halo(kind, source, target, axis, step):
        return remote(
            kv.at[source, kind], kv.at[target, kind],
            halo_s.at[kind, target], halo_r.at[kind, target], {axis: ahead(axis, step)},
        )

    def spread(kind, r):
        buf = (qs, gs)[kind]
        return remote(
            buf.at[own], buf.at[pl.ds(POS[r] * CELLS, CELLS)],
            ta_s.at[kind, r - 1], ta_r.at[kind, r - 1], {"ta": ahead("ta", -r)},
        )

    sent = []

    def go(copy):
        copy.start()
        sent.append(copy)
        return copy

    for kind in (0, 1):
        w_copies = [go(halo(kind, 4, 3, "wa", 1)), go(halo(kind, 4, 5, "wa", -1))]
        go(halo(kind, 4, 1, "ha", 1))
        go(halo(kind, 4, 7, "ha", -1))
        if kind == 0:
            q_copies = [go(spread(0, r)) for r in (2, 1, 3)]
    for kind in (0, 1):
        halo(kind, 4, 3, "wa", 1).wait_recv()
        go(halo(kind, 3, 0, "ha", 1))
        go(halo(kind, 3, 6, "ha", -1))
        halo(kind, 4, 5, "wa", -1).wait_recv()
        go(halo(kind, 5, 2, "ha", 1))
        go(halo(kind, 5, 8, "ha", -1))
    g_copies = [go(spread(1, r)) for r in (2, 1, 3)]

    def hidden(slot):
        row = h_pos + slot // 3 - 1
        col = w_pos + slot % 3 - 1
        shown = (row >= 0) & (row < h_size) & (col >= 0) & (col < w_size)
        return jnp.where(shown, 0.0, BIG)

    for copy in q_copies:
        copy.wait_recv()
    for kind in (0, 1):
        for target in (1, 7, 0, 6, 2, 8):
            halo(kind, 4, target, "ha", 1).wait_recv()

    o_copies = []
    for group in range(2):
        queries = pl.ds(group * PAIR, PAIR)
        rows = []
        for idx in range(HEADS):

            def first(slot, best):
                tile = dot_nt(kv[slot, 0, :, head(idx)], qs[queries, head(idx)])
                scores[slot] = tile
                return jnp.maximum(best, jnp.max(tile.reshape(CELLS // 8, 8, PAIR), axis=0) - hidden(slot))

            best = lax.fori_loop(0, 9, first, jnp.full((8, PAIR), -BIG, jnp.float32))
            best = jnp.max(best, axis=0, keepdims=True)
            acc_t[...] = jnp.zeros_like(acc_t)

            def second(slot, total):
                tile = jnp.exp2((scores[slot] - (best + hidden(slot))) * EXP2_SCALE)
                tile16 = tile.astype(jnp.bfloat16)
                probs[idx, slot, :, queries] = tile16
                acc_t[...] += dot_tn(kv[slot, 1, :, head(idx)], tile16)
                return total + jnp.sum(tile.reshape(CELLS // 8, 8, PAIR), axis=0)

            total = lax.fori_loop(0, 9, second, jnp.zeros((8, PAIR), jnp.float32))
            total = jnp.sum(total, axis=0, keepdims=True)
            mrow[group, idx : idx + 1, :] = best * SCALE
            rows.append(best * SCALE + jnp.log(total))
            osend[queries, head(idx)] = jnp.transpose(acc_t[...] / total).astype(jnp.bfloat16)
        lsend[group] = jnp.concatenate(rows + [jnp.zeros((6, PAIR), jnp.float32)], axis=0)
        for r in ((2, 1), (3,))[group]:
            back = 4 - r
            dest = {"ta": ahead("ta", r)}
            o_copies.append(go(remote(
                osend.at[pl.ds(POS[r] * CELLS, CELLS)], orecv.at[back - 1],
                o_s.at[back - 1], o_r.at[back - 1], dest)))
            o_copies.append(go(remote(
                lsend.at[group], lrecv.at[back - 1], l_s.at[back - 1], l_r.at[back - 1], dest)))

    for copy in o_copies:
        copy.wait_recv()
    parts = [pltpu.roll(lsend[1], CELLS, 1), lrecv[0], lrecv[1], pltpu.roll(lrecv[2], CELLS, 1)]
    top = jnp.maximum(jnp.maximum(parts[0], parts[1]), jnp.maximum(parts[2], parts[3]))
    weights = [jnp.exp(piece - top) for piece in parts]
    denom = weights[0] + weights[1] + weights[2] + weights[3]
    lse = top + jnp.log(denom)
    wide = jnp.concatenate([piece / denom for piece in weights] + [jnp.zeros((96, PAIR), jnp.float32)], axis=0)
    columns = jnp.transpose(wide)[:CELLS]
    deltas = []
    for idx in range(HEADS):
        total = columns[:, idx : idx + 1] * osend[own, head(idx)].astype(jnp.float32)
        for src in range(3):
            at = 8 * (src + 1) + idx
            total = total + columns[:, at : at + 1] * orecv[src, :, head(idx)].astype(jnp.float32)
        rounded = total.astype(jnp.bfloat16)
        o_ref[:, head(idx)] = rounded
        product = rounded.astype(jnp.float32) * g_ref[:, head(idx)].astype(jnp.float32)
        product = jnp.concatenate([product, product], axis=0)
        deltas.append(jnp.sum(jnp.transpose(product), axis=0, keepdims=True))
    lane_pair = lax.broadcasted_iota(jnp.int32, (8, PAIR), 1)
    sub_pair = lax.broadcasted_iota(jnp.int32, (8, PAIR), 0)
    twice = jnp.where(lane_pair < CELLS, lse, pltpu.roll(lse, CELLS, 1))
    stats = jnp.where(
        sub_pair < 2, twice,
        jnp.where(sub_pair == 2, jnp.broadcast_to(deltas[0], (8, PAIR)), jnp.broadcast_to(deltas[1], (8, PAIR))),
    )
    ssend[...] = stats
    st_copies = []
    for r in (2, 1, 3):
        st_copies.append(go(remote(ssend, srecv.at[r - 1], st_s.at[r - 1], st_r.at[r - 1], {"ta": ahead("ta", -r)})))
    for copy in st_copies + g_copies:
        copy.wait_recv()

    low = lane_pair < CELLS
    stat_rows = [jnp.where(low, srecv[1], srecv[0]), jnp.where(low, srecv[2], ssend[...])]
    factor_rows = [jnp.exp(mrow[group] - stat_rows[group]) for group in range(2)]
    dq_t[...] = jnp.zeros_like(dq_t)

    def backward(slot):
        for idx in range(HEADS):
            keys, values = kv[slot, 0, :, head(idx)], kv[slot, 1, :, head(idx)]
            for group in range(2):
                queries = pl.ds(group * PAIR, PAIR)
                pgrad = dot_nt(values, gs[queries, head(idx)])
                prob = probs[idx, slot, :, queries].astype(jnp.float32) * factor_rows[group][idx : idx + 1]
                probs[idx, slot, :, queries] = prob.astype(jnp.bfloat16)
                dtile = (prob * (pgrad - stat_rows[group][2 + idx : 3 + idx])).astype(jnp.bfloat16)
                dsc[:, queries] = dtile
                dq_t[idx, :, queries] += dot_tn(keys, dtile)
            part[slot, 0, :, head(idx)] = (dot_nn(dsc[...], qs[:, head(idx)]) * SCALE).astype(jnp.bfloat16)
            part[slot, 1, :, head(idx)] = dot_nn(probs[idx, slot], gs[:, head(idx)]).astype(jnp.bfloat16)

    def to_row(step):
        side = step % 2
        col = (step // 2) * 2 % 3
        return remote(
            part.at[side * 6 + col], hrecv.at[col, 1 - side], h_s.at[col, 1 - side], h_r.at[col, 1 - side],
            {"ha": lax.rem(h_pos + 2 * side - 1 + h_size, h_size)},
        )

    def outer(step, carry):
        backward((step % 2) * 6 + (step // 2) * 2 % 3)
        to_row(step).start()
        return carry

    lax.fori_loop(0, 6, outer, 0)

    def inner(step, carry):
        backward(step)
        return carry

    lax.fori_loop(3, 6, inner, 0)

    for idx in range(HEADS):
        dqsend[:, head(idx)] = jnp.transpose(dq_t[idx] * SCALE).astype(jnp.bfloat16)
    dq_copies = []
    for r in (2, 1, 3):
        back = 4 - r
        dq_copies.append(go(remote(
            dqsend.at[pl.ds(POS[r] * CELLS, CELLS)], dqrecv.at[back - 1],
            dq_s.at[back - 1], dq_r.at[back - 1], {"ta": ahead("ta", r)})))

    w_copies = []
    for number, col in enumerate((0, 2)):
        for step in (2 * number, 2 * number + 1):
            to_row(step).wait_recv()
        for kind in range(2):
            wsend[number, kind] = (
                part[3 + col, kind].astype(jnp.float32)
                + hrecv[col, 0, kind].astype(jnp.float32)
                + hrecv[col, 1, kind].astype(jnp.float32)
            ).astype(jnp.bfloat16)
        w_copies.append(go(remote(
            wsend.at[number], wrecv.at[number], w_s.at[number], w_r.at[number], {"wa": ahead("wa", col - 1)})))
    for step in (4, 5):
        to_row(step).wait_recv()

    for copy in dq_copies:
        copy.wait_recv()
    for idx in range(HEADS):
        total = dqsend[own, head(idx)].astype(jnp.float32)
        for src in range(3):
            total = total + dqrecv[src, :, head(idx)].astype(jnp.float32)
        dq_ref[:, head(idx)] = turn(total, cos_tab[...], sin_tab[...], -1.0).astype(jnp.bfloat16)
    for copy in w_copies:
        copy.wait_recv()
    for kind, out in ((0, dk_ref), (1, dv_ref)):
        for idx in range(HEADS):
            total = part[4, kind, :, head(idx)].astype(jnp.float32)
            for side in range(2):
                total = total + hrecv[1, side, kind, :, head(idx)].astype(jnp.float32)
                total = total + wrecv[side, kind, :, head(idx)].astype(jnp.float32)
            if kind == 0:
                total = turn(total, cos_tab[...], sin_tab[...], -1.0)
            out[:, head(idx)] = total.astype(jnp.bfloat16)
    for step in range(6):
        to_row(step).wait_send()
    for copy in sent:
        copy.wait_send()


def shards(query_in, key_in, value_in, cotangent):
    time_dims = DH // 8
    space_dims = (DH - time_dims) // 2
    slower = 256.0 ** (-np.arange(0, time_dims, 2, dtype=np.float32) / np.float32(time_dims))
    faster = 256.0 ** (-np.arange(0, space_dims, 2, dtype=np.float32) / np.float32(space_dims))
    freq = np.repeat(np.concatenate([slower, faster, faster]).astype(np.float32), 2)
    freq = np.broadcast_to(freq[None, :], (TILE, DH))
    shape = query_in.shape
    bf16, f32 = jnp.bfloat16, jnp.float32
    block = (CELLS, CHAN)
    dma = pltpu.SemaphoreType.DMA
    outs = pl.pallas_call(
        kernel,
        out_shape=[jax.ShapeDtypeStruct(block, bf16)] * 4,
        in_specs=[pl.BlockSpec(memory_space=pltpu.VMEM)] * 5,
        out_specs=[pl.BlockSpec(memory_space=pltpu.VMEM)] * 4,
        scratch_shapes=[
            pltpu.VMEM((9, 2) + block, bf16),
            pltpu.VMEM((QUERIES, CHAN), bf16),
            pltpu.VMEM((QUERIES, CHAN), bf16),
            pltpu.VMEM((CELLS, DH), f32),
            pltpu.VMEM((CELLS, DH), f32),
            pltpu.VMEM((9, CELLS, PAIR), f32),
            pltpu.VMEM((HEADS, 9, CELLS, QUERIES), bf16),
            pltpu.VMEM((CELLS, QUERIES), bf16),
            pltpu.VMEM((DH, PAIR), f32),
            pltpu.VMEM((HEADS, DH, QUERIES), f32),
            pltpu.VMEM((2, 8, PAIR), f32),
            pltpu.VMEM((QUERIES, CHAN), bf16),
            pltpu.VMEM((3,) + block, bf16),
            pltpu.VMEM((2, 8, PAIR), f32),
            pltpu.VMEM((3, 8, PAIR), f32),
            pltpu.VMEM((8, PAIR), f32),
            pltpu.VMEM((3, 8, PAIR), f32),
            pltpu.VMEM((QUERIES, CHAN), bf16),
            pltpu.VMEM((3,) + block, bf16),
            pltpu.VMEM((9, 2) + block, bf16),
            pltpu.VMEM((3, 2, 2) + block, bf16),
            pltpu.VMEM((2, 2) + block, bf16),
            pltpu.VMEM((2, 2) + block, bf16),
            dma((2, 9)), dma((2, 9)), dma((2, 3)), dma((2, 3)),
            dma((3,)), dma((3,)), dma((3,)), dma((3,)), dma((3,)), dma((3,)), dma((3,)), dma((3,)),
            dma((3, 2)), dma((3, 2)), dma((2,)), dma((2,)),
        ],
        compiler_params=pltpu.CompilerParams(collective_id=0, has_side_effects=True),
    )(jnp.asarray(freq), *(arg.reshape(block) for arg in (query_in, key_in, value_in, cotangent)))
    return tuple(out.reshape(shape) for out in outs)


def solution(mesh):
    spec = P("ta", "ha", "wa", None)
    return jax.shard_map(shards, mesh=mesh, in_specs=(spec,) * 4, out_specs=(spec,) * 4, check_vma=False)
```

profile of v0, /device:TPU:1, one launch (start us, length us, event | category | flops | bytes accessed | tf_op | source)
XLA Modules:
  0.0 100.9 jit_solution(2714027551782977234)
XLA Ops:
  0.6 0.0 copy-start.3
  0.6 0.6 copy-done.3
  1.3 0.6 jit_solution_.3.freq_ref
  1.9 94.9 %shard_map.84 = (bf16[192,256]{1,0:T(8,128)(2,1)}, bf16[192,256]{1,0:T(8,128)(2,1)}, bf16[192,256]{1,0:T(8,128)(2,1)}, bf16[192,256]{1,0:T(8,128)(2,1)}) custom-call(f32[8,128]{1,0:T(8,128)} %jit_solution_.3.freq_ref, bf16[192,256]{1,0:T(8,128)(2,1)} %bitcast.12, bf16[192,256]{1,0:T(8,128)(2,1)} %bitcast.13, bf16[192,256]{1,0:T(8,128)(2,1)} %bitcast.14, ...), custom_call_target="tpu_custom_call" | custom-call | tf_op jit(solution)/shard_map/pallas_call | solution.py:318
  96.8 0.0 copy-start.2
  96.8 1.6 %copy.13 = bf16[3,8,8,256]{3,2,1,0:T(8,128)(2,1)} copy(bf16[3,8,8,256]{3,2,1,0:T(8,128)(2,1)} %bitcast.11) | data formatting | bytes 196608
  98.4 0.0 copy-done.2
  98.4 0.0 copy-start.1
  98.4 0.6 copy.14
  99.0 0.3 copy-done.1
  99.3 0.0 copy-start
  99.3 0.6 copy.15
  100.0 0.3 copy-done
  100.3 0.6 copy.16
Async XLA Ops:
  0.6 0.7 copy-start.3
  96.8 1.6 %copy-start.2 = (bf16[192,256]{1,0:T(8,128)(2,1)S(1)}, bf16[192,256]{1,0:T(8,128)(2,1)}, u32[]{:S(2)}) copy-start(bf16[192,256]{1,0:T(8,128)(2,1)} %get-tuple-element.9) | copy-start | bytes 294916
  98.4 0.9 copy-start.1
  99.3 0.9 copy-start
where the time goes:
time: 101 us
  Pallas kernels  94.9 us (94%)
  local copies, waits for them, and re-layouts  5.32 us (5%)
    pallas_call x1, Pallas kernels, shards(): pl.pallas_call(kernel, out_shape=[jax.ShapeDtypeStruct(block, bf16)] * 4,...  94.9 us
    unnamed x12, local copies, waits for them, and re-layouts  4.72 us

commit v1 on v0

v1 whole, which is shorter than its diff:
```python
import functools

import jax
import jax.numpy as jnp
from jax import lax
from jax.experimental import pallas as pl
from jax.experimental.pallas import tpu as pltpu
from jax.sharding import PartitionSpec as P

DH = 128
HEADS = 2
TILE = 8
FRAMES = 3
CELLS = FRAMES * TILE * TILE
CHAN = HEADS * DH
HALF = CELLS // 2
PAIR = 2 * CELLS
QUERIES = 4 * CELLS
SCALE = DH ** (-0.5)
EXP2_SCALE = SCALE * 1.4426950408889634
BIG = 1e30
POS = {2: 0, 1: 1, 3: 2, 0: 3}


def ahead(axis, step):
    size = lax.axis_size(axis)
    return lax.rem(lax.axis_index(axis) + (step + size), size)


def dot_nt(a, b):
    return lax.dot_general(a, b, (((1,), (1,)), ((), ())), preferred_element_type=jnp.float32)


def dot_tn(a, b):
    return lax.dot_general(a, b, (((0,), (0,)), ((), ())), preferred_element_type=jnp.float32)


def dot_nn(a, b):
    return lax.dot_general(a, b, (((1,), (0,)), ((), ())), preferred_element_type=jnp.float32)


def turn(block, cosine, sine, direction):
    lane = lax.broadcasted_iota(jnp.int32, (CELLS, DH), 1)
    nxt = pltpu.roll(block, DH - 1, 1)
    prv = pltpu.roll(block, 1, 1)
    swapped = jnp.where(lane % 2 == 0, -nxt, prv)
    return block * cosine + swapped * (direction * sine)


def head(idx):
    return pl.ds(idx * DH, DH)


def kernel(
    q_ref, k_ref, v_ref, g_ref,
    o_ref, dq_ref, dk_ref, dv_ref,
    kv, qs, gs, cos_tab, sin_tab, scores, probs, pgrads, dsc, acc_t, dq_t, mrow,
    osend, orecv, orelay, ssend, srecv, dqsend, dqrecv, dqrelay,
    part, hrecv, wsend, wrecv,
    halo_s, halo_r, ta_s, ta_r, o_s, o_r, st_s, st_r, dq_s, dq_r, h_s, h_r, w_s, w_r,
):
    t_pos, h_pos, w_pos = lax.axis_index("ta"), lax.axis_index("ha"), lax.axis_index("wa")
    h_size, w_size = lax.axis_size("ha"), lax.axis_size("wa")

    barrier = pltpu.get_barrier_semaphore()
    odd = lax.rem(w_pos, 2)
    pair_w = {"wa": w_pos + 1 - 2 * odd}
    far_w = {"wa": lax.rem(w_pos + 2 - 4 * odd + w_size, w_size)}
    near_w = {"wa": lax.rem(w_pos - 2 + 4 * odd + w_size, w_size)}
    partners = [{"ha": ahead("ha", 1)}, {"ha": ahead("ha", -1)}, pair_w, far_w, near_w]
    partners += [{"ta": ahead("ta", r)} for r in (1, 2, 3)]
    for partner in partners:
        pl.semaphore_signal(barrier, inc=1, device_id=partner, device_id_type=pl.DeviceIdType.MESH)

    lane = lax.broadcasted_iota(jnp.int32, (TILE, DH), 1)
    sub = lax.broadcasted_iota(jnp.int32, (TILE, DH), 0)
    in_time = lane < DH // 8
    in_row = lane < DH // 8 + (DH - DH // 8) // 2
    start = jnp.where(in_time, t_pos * FRAMES, jnp.where(in_row, h_pos * TILE, w_pos * TILE))
    pair = (lane // 2).astype(jnp.float32)
    time_dims, space_dims = DH // 8, (DH - DH // 8) // 2
    power = jnp.where(
        in_time, pair * (2.0 / time_dims),
        jnp.where(in_row, pair - time_dims // 2, pair - (time_dims + space_dims) // 2) * (2.0 / space_dims),
    )
    angle = (start + sub).astype(jnp.float32) * jnp.exp2(-8.0 * power)
    for table, value in ((cos_tab, jnp.cos(angle)), (sin_tab, jnp.sin(angle))):
        for frame in range(FRAMES):
            for row in range(TILE):
                table[pl.ds((frame * TILE + row) * TILE, TILE), :] = jnp.where(
                    in_time,
                    jnp.broadcast_to(value[frame : frame + 1], (TILE, DH)),
                    jnp.where(in_row, jnp.broadcast_to(value[row : row + 1], (TILE, DH)), value),
                )
    own = pl.ds(POS[0] * CELLS, CELLS)
    for idx in range(HEADS):
        cosine, sine = cos_tab[...], sin_tab[...]
        kv[4, 0, :, head(idx)] = turn(k_ref[:, head(idx)].astype(jnp.float32), cosine, sine, 1.0).astype(jnp.bfloat16)
        qs[own, head(idx)] = turn(q_ref[:, head(idx)].astype(jnp.float32), cosine, sine, 1.0).astype(jnp.bfloat16)
    kv[4, 1] = v_ref[...]
    gs[own, :] = g_ref[...]

    pl.semaphore_wait(barrier, len(partners))

    def remote(src, dst, send, recv, device):
        return pltpu.make_async_remote_copy(
            src_ref=src, dst_ref=dst, send_sem=send, recv_sem=recv,
            device_id=device, device_id_type=pl.DeviceIdType.MESH,
        )

    swap_slot, relay_slot = 5 - 2 * odd, 3 + 2 * odd

    def halo(kind, source, target, device):
        return remote(
            kv.at[source, kind], kv.at[target, kind], halo_s.at[kind, target], halo_r.at[kind, target], device,
        )

    def arrived(kind, target):
        halo(kind, 4, target, pair_w).wait_recv()

    def rows_of(r, part=None):
        if part is None:
            return pl.ds(POS[r] * CELLS, CELLS)
        return pl.ds(POS[r] * CELLS + part * HALF, HALF)

    def spread(kind, step):
        buf = (qs, gs)[kind]
        return remote(
            buf.at[own], buf.at[rows_of(4 - step if step > 0 else 1)],
            ta_s.at[kind, step], ta_r.at[kind, step], {"ta": ahead("ta", 1 if step == 1 else -1)},
        )

    def spread_on(kind, step):
        buf = (qs, gs)[kind]
        part = 0 if step == 1 else 1
        return remote(
            buf.at[rows_of(3 if step == 1 else 1, part)], buf.at[rows_of(2, part)],
            ta_s.at[kind, 2 + step], ta_r.at[kind, 2 + step], {"ta": ahead("ta", 1 if step == 1 else -1)},
        )

    sent = []

    def go(copy):
        copy.start()
        sent.append(copy)
        return copy

    def hidden(slot):
        row = h_pos + slot // 3 - 1
        col = w_pos + slot % 3 - 1
        shown = (row >= 0) & (row < h_size) & (col >= 0) & (col < w_size)
        return jnp.where(shown, 0.0, BIG)

    up_h, down_h = {"ha": ahead("ha", 1)}, {"ha": ahead("ha", -1)}

    def own_out(kind):
        go(halo(kind, 4, relay_slot, pair_w))
        go(halo(kind, 4, 1, up_h))
        go(halo(kind, 4, 7, down_h))
        for step in (1, 0):
            go(spread(kind, step))

    def swap_on(kind):
        arrived(kind, swap_slot)
        go(halo(kind, swap_slot, relay_slot, far_w))
        go(halo(kind, swap_slot, swap_slot - 3, up_h))
        go(halo(kind, swap_slot, swap_slot + 3, down_h))

    def relay_on(kind):
        arrived(kind, relay_slot)
        go(halo(kind, relay_slot, relay_slot - 3, up_h))
        go(halo(kind, relay_slot, relay_slot + 3, down_h))

    def chain_on(kind):
        for step in (1, 0):
            spread(kind, step).wait_recv()
            go(spread_on(kind, step))

    def all_in(kind):
        for target in (1, 7, 0, 6, 2, 8):
            arrived(kind, target)

    bests = {}

    def score_pass(group, idx):
        queries = pl.ds(group * PAIR, PAIR)

        def first(slot, best):
            tile = dot_nt(kv[slot, 0, :, head(idx)], qs[queries, head(idx)])
            scores[idx, slot] = tile
            return jnp.maximum(best, jnp.max(tile.reshape(CELLS // 8, 8, PAIR), axis=0) - hidden(slot))

        best = lax.fori_loop(0, 9, first, jnp.full((8, PAIR), -BIG, jnp.float32))
        bests[idx] = jnp.max(best, axis=0, keepdims=True)

    def prob_pass(group):
        queries = pl.ds(group * PAIR, PAIR)
        lses, deltas = [], []
        for idx in range(HEADS):
            best = bests[idx]

            def second(slot, sums):
                total, delta = sums
                tile = jnp.exp2((scores[idx, slot] - (best + hidden(slot))) * EXP2_SCALE)
                probs[idx, slot, :, queries] = tile.astype(jnp.bfloat16)
                pgrad = dot_nt(kv[slot, 1, :, head(idx)], gs[queries, head(idx)])
                pgrads[idx, slot, :, queries] = pgrad
                total = total + jnp.sum(tile.reshape(CELLS // 8, 8, PAIR), axis=0)
                delta = delta + jnp.sum((tile * pgrad).reshape(CELLS // 8, 8, PAIR), axis=0)
                return total, delta

            zero = jnp.zeros((8, PAIR), jnp.float32)
            total, delta = lax.fori_loop(0, 9, second, (zero, zero))
            total = jnp.sum(total, axis=0, keepdims=True)
            mrow[group, idx : idx + 1, :] = best * SCALE
            lses.append(best * SCALE + jnp.log(total))
            deltas.append(jnp.sum(delta, axis=0, keepdims=True) / total)
        ssend[group] = jnp.concatenate(lses + deltas + [jnp.zeros((4, PAIR), jnp.float32)], axis=0)
        for r in (2, 1, 3):
            go(stat_copy(group, r))

    def stat_copy(group, r):
        return remote(
            ssend.at[group], srecv.at[r - 1, group], st_s.at[group, r - 1], st_r.at[group, r - 1],
            {"ta": ahead("ta", -r)},
        )

    for kind in (0, 1):
        own_out(kind)
    swap_on(0)
    chain_on(0)
    relay_on(0)
    swap_on(1)
    all_in(0)
    score_pass(1, 0)
    relay_on(1)
    score_pass(1, 1)
    chain_on(1)
    all_in(1)
    prob_pass(1)
    for step in (1, 0):
        spread_on(0, step).wait_recv()
    score_pass(0, 0)
    score_pass(0, 1)
    for step in (1, 0):
        spread_on(1, step).wait_recv()
    prob_pass(0)

    acc_t[...] = jnp.zeros_like(acc_t)

    def third(slot, carry):
        for idx in range(HEADS):
            acc_t[idx] += dot_tn(kv[slot, 1, :, head(idx)], probs[idx, slot])
        return carry

    lax.fori_loop(0, 9, third, 0)

    for group in range(2):
        for r in (2, 1, 3):
            stat_copy(group, r).wait_recv()
    low = lax.broadcasted_iota(jnp.int32, (8, PAIR), 1) < CELLS
    factor_rows, delta_rows = [], []
    for group in range(2):
        mine = (2, 1) if group == 0 else (3, 0)
        pieces = []
        for src in range(4):
            halves = []
            for side in range(2):
                pos = POS[(mine[side] - src) % 4]
                rows = ssend[pos // 2] if src == 0 else srecv[src - 1, pos // 2]
                halves.append(rows if pos % 2 == side else pltpu.roll(rows, CELLS, 1))
            pieces.append(jnp.where(low, halves[0], halves[1]))
        top = jnp.maximum(jnp.maximum(pieces[0], pieces[1]), jnp.maximum(pieces[2], pieces[3]))[:HEADS]
        weights = [jnp.exp(piece[:HEADS] - top) for piece in pieces]
        denom = weights[0] + weights[1] + weights[2] + weights[3]
        delta = sum(weight * piece[HEADS : 2 * HEADS] for weight, piece in zip(weights, pieces)) / denom
        factor_rows.append(jnp.exp(mrow[group, :HEADS] - (top + jnp.log(denom))))
        delta_rows.append(delta)

    def ring(buf, relay, recv, send_sems, recv_sems):
        def half(step):
            part = 0 if step == 1 else 1
            return remote(
                buf.at[rows_of(2, part)], relay.at[part], send_sems.at[part], recv_sems.at[part],
                {"ta": ahead("ta", 1 if step == 1 else -1)},
            )

        def rest(step, part):
            r = 1 if step == 1 else 3
            return remote(
                buf.at[rows_of(r, part)], recv.at[step, pl.ds(part * HALF, HALF)],
                send_sems.at[2 + 2 * step + part], recv_sems.at[2 + 2 * step + part], {"ta": ahead("ta", r)},
            )

        def begin():
            for step in (1, 0):
                half(step).start()
            for step in (1, 0):
                rest(step, step).start()

        def merge():
            for step in (1, 0):
                part = 1 - step
                half(step).wait_recv()
                rows = rows_of(1 if step == 1 else 3, part)
                buf[rows, :] = (buf[rows, :].astype(jnp.float32) + relay[part].astype(jnp.float32)).astype(jnp.bfloat16)
            for step in (1, 0):
                rest(step, 1 - step).start()

        def finish():
            for step in (1, 0):
                for part in range(2):
                    rest(step, part).wait_recv()

        def leave():
            for step in (1, 0):
                half(step).wait_send()
                for part in range(2):
                    rest(step, part).wait_send()

        def total(idx):
            piece = buf[own, head(idx)].astype(jnp.float32)
            for src in range(2):
                piece = piece + recv[src, :, head(idx)].astype(jnp.float32)
            return piece

        return begin, merge, finish, leave, total

    o_ring = ring(osend, orelay, orecv, o_s, o_r)
    dq_ring = ring(dqsend, dqrelay, dqrecv, dq_s, dq_r)
    for idx in range(HEADS):
        for group in range(2):
            queries = pl.ds(group * PAIR, PAIR)
            weighted = acc_t[idx, :, queries] * factor_rows[group][idx : idx + 1]
            osend[queries, head(idx)] = jnp.transpose(weighted).astype(jnp.bfloat16)
    o_ring[0]()
    dq_t[...] = jnp.zeros_like(dq_t)

    def backward(slot):
        for idx in range(HEADS):
            keys = kv[slot, 0, :, head(idx)]
            for group in range(2):
                queries = pl.ds(group * PAIR, PAIR)
                prob = probs[idx, slot, :, queries].astype(jnp.float32) * factor_rows[group][idx : idx + 1]
                probs[idx, slot, :, queries] = prob.astype(jnp.bfloat16)
                dtile = prob * (pgrads[idx, slot, :, queries] - delta_rows[group][idx : idx + 1])
                dsc[:, queries] = dtile.astype(jnp.bfloat16)
            dq_t[idx] += dot_tn(keys, dsc[...])
            part[slot, 0, :, head(idx)] = (dot_nn(dsc[...], qs[:, head(idx)]) * SCALE).astype(jnp.bfloat16)
            part[slot, 1, :, head(idx)] = dot_nn(probs[idx, slot], gs[:, head(idx)]).astype(jnp.bfloat16)

    def column(turn_idx):
        return jnp.where(turn_idx == 0, 2 * odd, jnp.where(turn_idx == 1, 2 - 2 * odd, 1))

    def to_row(turn_idx, side):
        return remote(
            part.at[side * 6 + column(turn_idx)], hrecv.at[turn_idx, 1 - side],
            h_s.at[turn_idx, 1 - side], h_r.at[turn_idx, 1 - side],
            {"ha": lax.rem(h_pos + 2 * side - 1 + h_size, h_size)},
        )

    def along_y():
        return remote(wsend.at[0], wrecv.at[0], w_s.at[0], w_r.at[0], near_w)

    def along_z():
        return remote(wsend.at[1], wrecv.at[1], w_s.at[1], w_r.at[1], pair_w)

    def gather_rows(turn_idx, kind):
        return (
            part[3 + column(turn_idx), kind].astype(jnp.float32)
            + hrecv[turn_idx, 0, kind].astype(jnp.float32)
            + hrecv[turn_idx, 1, kind].astype(jnp.float32)
        )

    def outer(step, carry):
        turn_idx, place = step // 3, step % 3
        backward(place * 2 % 3 * 3 + column(turn_idx))

        @pl.when(place < 2)
        def _():
            to_row(turn_idx, place).start()

        @pl.when(step == 2)
        def _():
            o_ring[1]()

        @pl.when(step == 3)
        def _():
            for side in range(2):
                to_row(0, side).wait_recv()
            for kind in range(2):
                wsend[0, kind] = gather_rows(0, kind).astype(jnp.bfloat16)
            along_y().start()

        return carry

    lax.fori_loop(0, 9, outer, 0)

    for idx in range(HEADS):
        dqsend[:, head(idx)] = jnp.transpose(dq_t[idx] * SCALE).astype(jnp.bfloat16)

    dq_ring[0]()

    for side in range(2):
        to_row(1, side).wait_recv()
    along_y().wait_recv()
    for kind in range(2):
        wsend[1, kind] = (gather_rows(1, kind) + wrecv[0, kind].astype(jnp.float32)).astype(jnp.bfloat16)
    along_z().start()
    dq_ring[1]()

    o_ring[2]()
    for idx in range(HEADS):
        o_ref[:, head(idx)] = o_ring[4](idx).astype(jnp.bfloat16)
    for side in range(2):
        to_row(2, side).wait_recv()
    dq_ring[2]()
    for idx in range(HEADS):
        dq_ref[:, head(idx)] = turn(dq_ring[4](idx), cos_tab[...], sin_tab[...], -1.0).astype(jnp.bfloat16)
    along_z().wait_recv()
    for kind, out in ((0, dk_ref), (1, dv_ref)):
        for idx in range(HEADS):
            total = part[4, kind, :, head(idx)].astype(jnp.float32)
            for side in range(2):
                total = total + hrecv[2, side, kind, :, head(idx)].astype(jnp.float32)
            total = total + wrecv[1, kind, :, head(idx)].astype(jnp.float32)
            if kind == 0:
                total = turn(total, cos_tab[...], sin_tab[...], -1.0)
            out[:, head(idx)] = total.astype(jnp.bfloat16)
    for turn_idx in range(3):
        for side in range(2):
            to_row(turn_idx, side).wait_send()
    along_y().wait_send()
    along_z().wait_send()
    o_ring[3]()
    dq_ring[3]()
    for copy in sent:
        copy.wait_send()


def shards(query_in, key_in, value_in, cotangent):
    shape = query_in.shape
    bf16, f32 = jnp.bfloat16, jnp.float32
    block = (CELLS, CHAN)
    dma = pltpu.SemaphoreType.DMA
    outs = pl.pallas_call(
        kernel,
        out_shape=[jax.ShapeDtypeStruct(block, bf16)] * 4,
        in_specs=[pl.BlockSpec(memory_space=pltpu.VMEM)] * 4,
        out_specs=[pl.BlockSpec(memory_space=pltpu.VMEM)] * 4,
        scratch_shapes=[
            pltpu.VMEM((9, 2) + block, bf16),
            pltpu.VMEM((QUERIES, CHAN), bf16),
            pltpu.VMEM((QUERIES, CHAN), bf16),
            pltpu.VMEM((CELLS, DH), f32),
            pltpu.VMEM((CELLS, DH), f32),
            pltpu.VMEM((HEADS, 9, CELLS, PAIR), f32),
            pltpu.VMEM((HEADS, 9, CELLS, QUERIES), bf16),
            pltpu.VMEM((HEADS, 9, CELLS, QUERIES), f32),
            pltpu.VMEM((CELLS, QUERIES), bf16),
            pltpu.VMEM((HEADS, DH, QUERIES), f32),
            pltpu.VMEM((HEADS, DH, QUERIES), f32),
            pltpu.VMEM((2, 8, PAIR), f32),
            pltpu.VMEM((QUERIES, CHAN), bf16),
            pltpu.VMEM((2,) + block, bf16),
            pltpu.VMEM((2, HALF, CHAN), bf16),
            pltpu.VMEM((2, 8, PAIR), f32),
            pltpu.VMEM((3, 2, 8, PAIR), f32),
            pltpu.VMEM((QUERIES, CHAN), bf16),
            pltpu.VMEM((2,) + block, bf16),
            pltpu.VMEM((2, HALF, CHAN), bf16),
            pltpu.VMEM((9, 2) + block, bf16),
            pltpu.VMEM((3, 2, 2) + block, bf16),
            pltpu.VMEM((2, 2) + block, bf16),
            pltpu.VMEM((2, 2) + block, bf16),
            dma((2, 9)), dma((2, 9)), dma((2, 4)), dma((2, 4)),
            dma((6,)), dma((6,)), dma((2, 3)), dma((2, 3)), dma((6,)), dma((6,)),
            dma((3, 2)), dma((3, 2)), dma((2,)), dma((2,)),
        ],
        compiler_params=pltpu.CompilerParams(collective_id=0, has_side_effects=True),
    )(*(arg.reshape(block) for arg in (query_in, key_in, value_in, cotangent)))
    return tuple(out.reshape(shape) for out in outs)


def solution(mesh):
    spec = P("ta", "ha", "wa", None)
    return jax.shard_map(shards, mesh=mesh, in_specs=(spec,) * 4, out_specs=(spec,) * 4, check_vma=False)
```

time: 101 us -> 79.7 us (0.79)
  Pallas kernels: 94.9 us -> 74.7 us
  local copies, waits for them, and re-layouts: 5.32 us -> 4.07 us
    pallas_call x1, Pallas kernels: 94.9 us -> 74.7 us  [shards(): pl.pallas_call(kernel, out_shape=[jax.ShapeDtypeStruct(block, bf16)] * 4,...]
    unnamed x12 -> x10, local copies, waits for them, and re-layouts: 4.72 us -> 4.07 us
where the time goes in v1:
time: 79.7 us; the launch traced here: 79.4 us
  Pallas kernels  74.7 us (94%)
  local copies, waits for them, and re-layouts  4.07 us (5%)
    pallas_call x1, Pallas kernels, shards(): pl.pallas_call(kernel, out_shape=[jax.ShapeDtypeStruct(block, bf16)] * 4,...  74.7 us
    unnamed x10, local copies, waits for them, and re-layouts  4.07 us

profile of v1, /device:TPU:1, one launch (start us, length us, event | category | flops | bytes accessed | tf_op | source)
XLA Modules:
  0.0 79.4 jit_solution(1941091127857936626)
XLA Ops:
  0.6 74.7 %shard_map.75 = (bf16[192,256]{1,0:T(8,128)(2,1)}, bf16[192,256]{1,0:T(8,128)(2,1)}, bf16[192,256]{1,0:T(8,128)(2,1)}, bf16[192,256]{1,0:T(8,128)(2,1)}) custom-call(bf16[192,256]{1,0:T(8,128)(2,1)} %bitcast.12, bf16[192,256]{1,0:T(8,128)(2,1)} %bitcast.13, bf16[192,256]{1,0:T(8,128)(2,1)} %bitcast.14, bf16[192,256]{1,0:T(8,128)(2,1)} %bitcast.15), custom_call_target="tpu_custom_call" | custom-call | tf_op jit(solution)/shard_map/pallas_call | solution.py:446
  75.3 0.0 copy-start.2
  75.3 1.6 %copy.12 = bf16[3,8,8,256]{3,2,1,0:T(8,128)(2,1)} copy(bf16[3,8,8,256]{3,2,1,0:T(8,128)(2,1)} %bitcast.11) | data formatting | bytes 196608
  76.9 0.0 copy-done.2
  76.9 0.0 copy-start.1
  76.9 0.6 copy.13
  77.5 0.3 copy-done.1
  77.8 0.0 copy-start
  77.8 0.6 copy.14
  78.5 0.3 copy-done
  78.7 0.6 copy.15
Async XLA Ops:
  75.3 1.6 %copy-start.2 = (bf16[192,256]{1,0:T(8,128)(2,1)S(1)}, bf16[192,256]{1,0:T(8,128)(2,1)}, u32[]{:S(2)}) copy-start(bf16[192,256]{1,0:T(8,128)(2,1)} %get-tuple-element.9) | copy-start | bytes 294916
  76.9 0.9 %copy-start.1 = (bf16[192,256]{1,0:T(8,128)(2,1)S(1)}, bf16[192,256]{1,0:T(8,128)(2,1)}, u32[]{:S(2)}) copy-start(bf16[192,256]{1,0:T(8,128)(2,1)} %get-tuple-element.10) | copy-start | bytes 294916
  77.8 0.9 %copy-start = (bf16[192,256]{1,0:T(8,128)(2,1)S(1)}, bf16[192,256]{1,0:T(8,128)(2,1)}, u32[]{:S(2)}) copy-start(bf16[192,256]{1,0:T(8,128)(2,1)} %get-tuple-element.11) | copy-start | bytes 294916
